TPU v7x, 256 devices: a whole 4x4x8 slice. The times are simulated.
256 devices in a mesh: section: 16 (over x, y_lo, core), dp: 8 (over z), tensor: 2 (over y_hi).
Axes of the slice: x: 4, y: 4 (y_hi: 2, y_lo: 2; y = y_hi * 2 + y_lo), z: 8, core: 2. Of those that a mesh axis runs over, the one named last changes fastest.
Arguments:
- activations: bfloat16 [16, 8192, 2048], P('section', 'dp', 'tensor'), may hold values from -150 to 150, as said below
- sent_grads: bfloat16 [16, 8192, 2048], P('section', 'dp', 'tensor'), may hold values from -150 to 150, as said below
- damping: float32 [16, 2, 2], P('section', None, 'tensor'), may hold values from 0.05 to 0.5
- bubble_steps: int32 [16, 2, 2], P('section', None, 'tensor'), may hold values from 1 to 3
- warm: float32 [16, 2, 2, 1024, 1024], P('section', None, 'tensor', 'dp'), may hold values from -0.02 to 1.2, as said below
Outputs:
- inverse: float32 [16, 2, 2, 1024, 1024], P('section', None, 'tensor', 'dp')
Inputs may be any that keep to these rules, and one draw needn't show every extreme that they name: `activations`: input features of one section's layer, rows and columns of differing scales. `sent_grads`: gradients of one section's layer outputs, rows and columns of differing scales. `warm`: symmetric with a positive diagonal; Newton-Schulz steps from it contract toward the inverse of each block's factor.
All inputs are finite; a program needn't handle non-finite values.
Results may differ from a plain program's by a relative error of at most 0.0003.
Values may be sent and summed in bfloat16 or wider, within the bound.
A program may use at most 192 MiB of HBM per device.

v0:
```python
import jax
import jax.numpy as jnp
from jax import lax
from jax.sharding import PartitionSpec as P

ITERS = 3


def from_behind(value, axis, steps):
    count = lax.axis_size(axis)
    leading, last = (max(0, -steps), min(count, count - steps))
    return lax.ppermute(value, axis, [(source, source + steps) for source in range(leading, last)])


def gram(rows):
    return lax.dot_general(rows, rows, (((0,), (0,)), ((), ())), preferred_element_type=jnp.float32)


def fetch_grads(sent_grads):
    return from_behind(sent_grads, "section", -1)


def newton_step(iterates, factors, counts, index):
    products = tuple(
        (jnp.dot(x, f, precision=lax.Precision.HIGHEST) for x, f in zip(iterates, factors))
    )
    pieces = jax.tree.map(lambda part: lax.all_gather(part, "dp", axis=0, tiled=True), iterates)
    folded = tuple(
        (
            jnp.dot(product, piece, precision=lax.Precision.HIGHEST)
            for product, piece in zip(products, pieces)
        )
    )
    return tuple(
        (jnp.where(index < count, 2.0 * x - t, x) for x, t, count in zip(iterates, folded, counts))
    )


def local(activations, sent_grads, damping, bubble_steps, warm):
    inputs = activations[0]
    received = fetch_grads(sent_grads)
    first_part = gram(inputs)
    second_part = gram(received[0])
    first_sum, second_sum = lax.psum((first_part, second_part), "dp")
    total_tokens = inputs.shape[0] * lax.axis_size("dp")
    identity = jnp.eye(first_sum.shape[0], dtype=jnp.float32)
    factors = (
        first_sum / total_tokens + damping[0, 0, 0] * identity,
        second_sum / total_tokens + damping[0, 1, 0] * identity,
    )
    counts = (bubble_steps[0, 0, 0], bubble_steps[0, 1, 0])
    iterates = (warm[0, 0, 0], warm[0, 1, 0])
    for index in range(ITERS):
        iterates = newton_step(iterates, factors, counts, index)
    return jnp.stack(iterates)[None, :, None]


def solution(mesh):
    placed = (
        P("section", "dp", "tensor"),
        P("section", "dp", "tensor"),
        P("section", None, "tensor"),
        P("section", None, "tensor"),
        P("section", None, "tensor", "dp", None),
    )
    return jax.shard_map(
        local,
        mesh=mesh,
        in_specs=placed,
        out_specs=P("section", None, "tensor", "dp", None),
        check_vma=False,
    )
```

profile of v0, /device:TPU:16, one launch (start us, length us, event | category | flops | bytes accessed | tf_op | source)
XLA Modules:
  0.0 573.6 jit_solution(16592266944513606604)
XLA Ops:
  6.5 0.0 copy-start
  6.5 0.0 all-reduce.3.cloned.1.call-start
  6.5 1.4 collective-permute-start
  8.0 0.2 copy-done
  8.1 4.4 fusion.12
  12.5 0.4 collective-permute-done
  12.9 4.4 fusion.10
  17.3 0.0 all-reduce.3.cloned.1.call-update
  17.3 0.0 all-gather.17.cloned.1.call-start
  17.4 1.1 copy-done.5
  18.5 1.1 fusion.66
  19.6 0.0 all-gather.17.cloned.1.call-update
  19.6 0.0 all-gather.19.cloned.1.call-start
  19.6 0.7 all-gather.19.cloned.1.call-update
  20.3 0.2 all-gather.9.cloned.1.call-start
  20.6 0.0 copy-done.7
  20.6 0.6 fusion.67
  21.7 0.0 copy-done.8
  21.7 0.6 fusion.68
  22.3 207.5 %all-reduce.3.cloned.1.call-done = (f32[1024,1024]{1,0:T(8,128)}, f32[1024,1024]{1,0:T(8,128)}) async-done(((f32[1024,1024]{1,0:T(8,128)}, f32[1024,1024]{1,0:T(8,128)}), (f32[1024,1024]{1,0:T(8,128)}, f32[1024,1024]{1,0:T(8,128)})) %all-reduce.3.cloned.1.call-update) | async-done | bytes 8388624 | tf_op jit(solution)/shard_map/psum | solution.py:44
  229.8 10.3 %fusion.6 = f32[1024,128]{1,0:T(8,128)} fusion(f32[1024,1024]{1,0:T(8,128)} %get-tuple-element.6, f32[]{:T(128)} %bitcast.5, f32[1,2,1,128,1024]{4,3,2,1,0:T(8,128)S(1)} %copy-done.5), kind=kOutput, calls=%fused_computation.9 | convolution fusion | flops 1614807040 | bytes 5242884 | tf_op jit(solution)/shard_map/dot_general | solution.py:25
  240.1 45.1 %all-gather.17.cloned.1.call-done = f32[1,1,1,1024,1024]{4,3,2,1,0:T(8,128)} async-done(((f32[1,1,1,128,1024]{4,3,2,1,0:T(8,128)}), f32[1,1,1,1024,1024]{4,3,2,1,0:T(8,128)}) %all-gather.17.cloned.1.call-update) | async-done | bytes 4194320 | tf_op jit(solution)/shard_map/all_gather | solution.py:27
  285.1 5.5 fusion.35
  290.7 0.0 all-gather.9.cloned.1.call-update
  290.7 0.3 all-gather.13.cloned.1.call-start
  291.5 10.3 %fusion.9 = f32[1024,128]{1,0:T(8,128)} fusion(f32[1024,1024]{1,0:T(8,128)} %get-tuple-element.5, f32[]{:T(128)} %bitcast.13, f32[1,2,1,128,1024]{4,3,2,1,0:T(8,128)S(1)} %copy-done.5), kind=kOutput, calls=%fused_computation.12 | convolution fusion | flops 1614807040 | bytes 5242884 | tf_op jit(solution)/shard_map/dot_general | solution.py:25
  301.8 38.5 %all-gather.19.cloned.1.call-done = f32[1,1,1,1024,1024]{4,3,2,1,0:T(8,128)} async-done(((f32[1,1,1,128,1024]{4,3,2,1,0:T(8,128)}), f32[1,1,1,1024,1024]{4,3,2,1,0:T(8,128)}) %all-gather.19.cloned.1.call-update) | async-done | bytes 4194320 | tf_op jit(solution)/shard_map/all_gather | solution.py:27
  340.3 5.6 fusion.41
  345.9 0.0 all-gather.13.cloned.1.call-update
  346.0 0.0 all-gather.11.cloned.1.call-start
  346.6 6.2 %fusion.5 = f32[128,1024]{1,0:T(8,128)} fusion(f32[128,1024]{1,0:T(8,128)S(1)} %copy-done.2, f32[1024,1024]{1,0:T(8,128)} %get-tuple-element.6, f32[]{:T(128)} %bitcast.5), kind=kOutput, calls=%fused_computation.8 | convolution fusion | flops 1614807040 | bytes 5242884 | tf_op jit(solution)/shard_map/dot_general | solution.py:25
  352.8 42.6 %all-gather.9.cloned.1.call-done = f32[1024,1024]{1,0:T(8,128)} async-done(((f32[128,1024]{1,0:T(8,128)}), f32[1024,1024]{1,0:T(8,128)}) %all-gather.9.cloned.1.call-update) | async-done | bytes 4194320 | tf_op jit(solution)/shard_map/all_gather | solution.py:27
  395.3 5.6 fusion.49
  400.9 0.0 all-gather.11.cloned.1.call-update
  400.9 0.4 all-gather.15.cloned.1.call-start
  401.9 0.0 copy-done.3
  402.0 6.2 %fusion.8 = f32[128,1024]{1,0:T(8,128)} fusion(f32[128,1024]{1,0:T(8,128)S(1)} %copy-done.3, f32[1024,1024]{1,0:T(8,128)} %get-tuple-element.5, f32[]{:T(128)} %bitcast.13), kind=kOutput, calls=%fused_computation.11 | convolution fusion | flops 1614807040 | bytes 5242884 | tf_op jit(solution)/shard_map/dot_general | solution.py:25
  408.2 42.2 %all-gather.13.cloned.1.call-done = f32[1024,1024]{1,0:T(8,128)} async-done(((f32[128,1024]{1,0:T(8,128)}), f32[1024,1024]{1,0:T(8,128)}) %all-gather.13.cloned.1.call-update) | async-done | bytes 4194320 | tf_op jit(solution)/shard_map/all_gather | solution.py:27
  450.3 5.6 fusion.46
  455.9 0.0 all-gather.15.cloned.1.call-update
  457.6 6.2 %fusion.4 = f32[128,1024]{1,0:T(8,128)} fusion(f32[128,1024]{1,0:T(8,128)S(1)} %copy-done.1, f32[1024,1024]{1,0:T(8,128)} %get-tuple-element.6, f32[]{:T(128)} %bitcast.5), kind=kOutput, calls=%fused_computation.7 | convolution fusion | flops 1614807040 | bytes 5242884 | tf_op jit(solution)/shard_map/dot_general | solution.py:25
  463.8 0.0 copy-done.4
  463.8 4.0 fusion.7
  467.8 37.6 %all-gather.11.cloned.1.call-done = f32[1024,1024]{1,0:T(8,128)} async-done(((f32[128,1024]{1,0:T(8,128)}), f32[1024,1024]{1,0:T(8,128)}) %all-gather.11.cloned.1.call-update) | async-done | bytes 4194320 | tf_op jit(solution)/shard_map/all_gather | solution.py:27
  505.4 5.6 fusion.48
  511.0 49.6 %all-gather.15.cloned.1.call-done = f32[1024,1024]{1,0:T(8,128)} async-done(((f32[128,1024]{1,0:T(8,128)}), f32[1024,1024]{1,0:T(8,128)}) %all-gather.15.cloned.1.call-update) | async-done | bytes 4194320 | tf_op jit(solution)/shard_map/all_gather | solution.py:27
  560.7 4.8 fusion.45
  565.5 1.0 maximum_bitcast_fusion
  (13 shorter events, 0.0 us)
Async XLA Ops:
  6.5 1.6 copy-start
  6.5 223.2 %all-reduce.3.cloned.1.call-start = ((), (), s32[]{:S(2)}) async-start(), calls=%async_computation.6 | async-start | bytes 16777216 | tf_op jit(solution)/shard_map/psum | solution.py:44
  6.5 6.4 %collective-permute-start = (bf16[1,1024,1024]{2,1,0:T(8,128)(2,1)}, bf16[1,1024,1024]{2,1,0:T(8,128)(2,1)S(1)}, u32[]{:S(2)}, u32[]{:S(2)}) collective-permute-start(bf16[1,1024,1024]{2,1,0:T(8,128)(2,1)} %param.6), channel_id=1, source_target_pairs={{16,0},{32,16},{48,32},{64,48},{80,64},{96,80},{112,96},{128,112},... | collective-permute-start | bytes 6291464 | tf_op jit(solution)/shard_map/ppermute | solution.py:12
  17.3 1.2 copy-start.5
  17.3 3.3 copy-start.7
  17.3 4.4 copy-start.8
  17.3 267.8 %all-gather.17.cloned.1.call-start = ((), (), s32[]{:S(2)}) async-start(), calls=%async_computation.4 | async-start | bytes 4718592 | tf_op jit(solution)/shard_map/all_gather | solution.py:27
  19.6 320.7 %all-gather.19.cloned.1.call-start = ((), (), s32[]{:S(2)}) async-start(), calls=%async_computation.5 | async-start | bytes 4718592 | tf_op jit(solution)/shard_map/all_gather | solution.py:27
  20.3 375.0 %all-gather.9.cloned.1.call-start = ((), (), s32[]{:S(2)}) async-start(), calls=%async_computation | async-start | bytes 4718592 | tf_op jit(solution)/shard_map/all_gather | solution.py:27
  290.7 159.7 %all-gather.13.cloned.1.call-start = ((), (), s32[]{:S(2)}) async-start(), calls=%async_computation.2 | async-start | bytes 4718592 | tf_op jit(solution)/shard_map/all_gather | solution.py:27
  301.8 44.8 %copy-start.2 = (f32[128,1024]{1,0:T(8,128)S(1)}, f32[128,1024]{1,0:T(8,128)}, u32[]{:S(2)}) copy-start(f32[128,1024]{1,0:T(8,128)} %fusion.35) | copy-start | bytes 1572868
  346.0 159.4 %all-gather.11.cloned.1.call-start = ((), (), s32[]{:S(2)}) async-start(), calls=%async_computation.1 | async-start | bytes 4718592 | tf_op jit(solution)/shard_map/all_gather | solution.py:27
  352.8 49.2 %copy-start.3 = (f32[128,1024]{1,0:T(8,128)S(1)}, f32[128,1024]{1,0:T(8,128)}, u32[]{:S(2)}) copy-start(f32[128,1024]{1,0:T(8,128)} %fusion.41) | copy-start | bytes 1572868
  400.9 159.6 %all-gather.15.cloned.1.call-start = ((), (), s32[]{:S(2)}) async-start(), calls=%async_computation.3 | async-start | bytes 4718592 | tf_op jit(solution)/shard_map/all_gather | solution.py:27
  408.2 49.4 %copy-start.1 = (f32[128,1024]{1,0:T(8,128)S(1)}, f32[128,1024]{1,0:T(8,128)}, u32[]{:S(2)}) copy-start(f32[128,1024]{1,0:T(8,128)} %fusion.49) | copy-start | bytes 1572868
  455.9 7.9 %copy-start.4 = (f32[128,1024]{1,0:T(8,128)S(1)}, f32[128,1024]{1,0:T(8,128)}, u32[]{:S(2)}) copy-start(f32[128,1024]{1,0:T(8,128)} %fusion.46) | copy-start | bytes 1572868
  455.9 7.8 %copy-start.9 = (f32[1024,1024]{1,0:T(8,128)S(1)}, f32[1024,1024]{1,0:T(8,128)}, u32[]{:S(2)}) copy-start(f32[1024,1024]{1,0:T(8,128)} %get-tuple-element.5) | copy-start | bytes 12582916
  511.0 54.5 %copy-start.6 = (f32[1,128,1024]{2,1,0:T(8,128)S(1)}, f32[1,128,1024]{2,1,0:T(8,128)}, u32[]{:S(2)}) copy-start(f32[1,128,1024]{2,1,0:T(8,128)} %fusion.48) | copy-start | bytes 1572868
Sparse Core Ops, SparseCore 0:
  17.4 212.2 all-reduce.2
  231.6 53.4 all-gather.16
  286.9 53.3 all-gather.18
  341.9 53.3 all-gather.8
  397.0 53.3 all-gather.12
  452.0 53.3 all-gather.10
  507.2 53.3 all-gather.14
where the time goes:
time: 579 us; the launch traced here: 574 us
  waiting for transfers between devices  464 us (80%)
  matrix products  84.6 us (15%)
  between operations  17.8 us (3%)
    all_gather x6, waiting for transfers between devices, newton_step(): lax.all_gather(part, 'dp', axis=0, tiled=True)  255 us
    psum x1, waiting for transfers between devices, local(): first_sum, second_sum = lax.psum((first_part, second_part), 'dp')  207 us
    dot_general x6, matrix products, newton_step(): jnp.dot(x, f, precision=lax.Precision.HIGHEST)  43.1 us
    dot_general x6, matrix products, newton_step(): jnp.dot(product, piece, precision=lax.Precision.HIGHEST)  32.7 us
  transfers between devices with their start and end apart: 8, of which 8 were waited for; matrix products, arithmetic and copies ran while one was open for 14% of the time, Pallas kernels for 0%

commit v1 on v0

v1 whole, which is shorter than its diff:
```python
import functools

import jax
import jax.numpy as jnp
from jax import lax
from jax.experimental import pallas as pl
from jax.experimental.pallas import tpu as pltpu
from jax.sharding import PartitionSpec as P

MESH = pl.DeviceIdType.MESH
ITERS = 3
RING = 8
ROWS = 128
STRIP = 5
WIDE = STRIP * ROWS
HALF = ROWS // 2
LEVELS = 32767.0
TINY = 1e-30


def diagonal_mask():
    row = lax.broadcasted_iota(jnp.int32, (ROWS, ROWS), 0)
    column = lax.broadcasted_iota(jnp.int32, (ROWS, ROWS), 1)
    return row == column


def encode(strip, code_ref, side_ref):
    mask = diagonal_mask()
    square = strip[:, :ROWS]
    diagonal = jnp.where(mask, square, 0.0)
    along_lanes = jnp.sum(diagonal, axis=0, keepdims=True)
    along_rows = jnp.sum(diagonal, axis=1, keepdims=True)
    rest = jnp.concatenate([jnp.where(mask, 0.0, square), strip[:, ROWS:]], axis=1)
    scaled = rest / jnp.sqrt(jnp.maximum(along_rows, TINY))
    largest = jnp.maximum(jnp.max(jnp.abs(scaled), axis=0, keepdims=True), TINY)
    code_ref[...] = jnp.round(scaled * (LEVELS / largest)).astype(jnp.int32).astype(jnp.int16)
    largest = largest / LEVELS
    pieces = [largest[:, b * ROWS:(b + 1) * ROWS] for b in range(STRIP)]
    zero = jnp.zeros_like(along_lanes)
    side_ref[...] = jnp.concatenate(pieces + [along_lanes, zero, zero], axis=0)


def exchange_kernel(act, grad, warm, fs, fd, xs, xd, a, g, rb, qb, qd, in_sem, rs_send, rs_recv, ag_send, ag_recv, hop_sem):
    z = lax.axis_index("dp")
    s = lax.axis_index("section")
    sections = lax.axis_size("section")
    right, left = lax.rem(z + 1, RING), lax.rem(z + RING - 1, RING)
    before, behind = lax.rem(s + sections - 1, sections), lax.rem(s + 1, sections)
    width = act.shape[1]
    extra = WIDE - ROWS

    loads = []
    for m, source in enumerate((act, grad)):
        loads.append((
            pltpu.make_async_copy(source, a.at[m, :, pl.ds(0, width)], in_sem.at[m, 0]),
            pltpu.make_async_copy(source.at[:, pl.ds(0, extra)], a.at[m, :, pl.ds(width, extra)], in_sem.at[m, 1]),
        ))
        for copy in loads[-1]:
            copy.start()

    barrier = pltpu.get_barrier_semaphore()
    for target in ({"dp": right}, {"dp": left}, {"section": before}, {"section": behind}):
        pl.semaphore_signal(barrier, inc=1, device_id=target, device_id_type=MESH)

    for m in range(2):
        blocks = [
            warm[m, :, pl.ds(pl.multiple_of(lax.rem(z + b, RING) * ROWS, ROWS), ROWS)] for b in range(STRIP)
        ]
        encode(jnp.concatenate(blocks, axis=1), xs.at[m, z], xd.at[m, z])
    pl.semaphore_wait(barrier, 4)

    sent = []

    def start(copy):
        copy.start()
        sent.append(copy)

    def gram(m, owner):
        first = pl.multiple_of(owner * ROWS, ROWS)
        g[m, owner] = lax.dot_general(
            a[m, :, pl.ds(first, ROWS)], a[m, :, pl.ds(first, WIDE)],
            (((0,), (0,)), ((), ())), preferred_element_type=jnp.float32,
        )

    def reduce_copy(m, d, step, source):
        return pltpu.make_async_remote_copy(
            src_ref=source, dst_ref=rb.at[m, d, step], send_sem=rs_send.at[m, d, step], recv_sem=rs_recv.at[m, d, step],
            device_id={"dp": (right, left)[d]}, device_id_type=MESH,
        )

    def gather_copies(which, codes, sides, m, d, step, owner):
        rows = (pl.ds(0, ROWS), pl.ds(d * HALF, HALF))[step == RING // 2 - 1]
        target = {"dp": (right, left)[d]}
        code = codes.at[m, owner, rows]
        copies = [pltpu.make_async_remote_copy(
            src_ref=code, dst_ref=code, send_sem=ag_send.at[which, m, d, step, 0], recv_sem=ag_recv.at[which, m, d, step, 0],
            device_id=target, device_id_type=MESH,
        )]
        if step < RING // 2 - 1 or d == 0:
            side = sides.at[m, owner]
            copies.append(pltpu.make_async_remote_copy(
                src_ref=side, dst_ref=side, send_sem=ag_send.at[which, m, d, step, 1], recv_sem=ag_recv.at[which, m, d, step, 1],
                device_id=target, device_id_type=MESH,
            ))
        return copies

    def owner_of(d, distance):
        return lax.rem(z + (RING - distance, distance)[d], RING)

    def gather_start(which, codes, sides, m, step):
        for d in range(2):
            for copy in gather_copies(which, codes, sides, m, d, step, owner_of(d, step)):
                start(copy)

    def gather_wait(which, codes, sides, m, step):
        for d in range(2):
            for copy in gather_copies(which, codes, sides, m, d, step, owner_of(d, step + 1)):
                copy.wait_recv()

    for m in range(2):
        for copy in loads[m]:
            copy.wait()
        for d in range(2):
            owner = owner_of(d, 1)
            gram(m, owner)
            start(reduce_copy(m, d, 0, g.at[m, owner, pl.ds(d * HALF, HALF)]))
    for m in range(2):
        gather_start(0, xs, xd, m, 0)

    @pl.loop(0, RING - 2)
    def _(j):
        owner = lax.rem(z + 2 + j + j // (RING - 3), RING)
        for m in range(2):
            gram(m, owner)

    for step in range(RING - 1):
        for m in (1, 0):
            for d in range(2):
                slot = rb.at[m, d, step]
                reduce_copy(m, d, step, slot).wait_recv()
                owner = owner_of(d, (step + 2) % RING)
                slot[...] += g[m, owner, pl.ds(d * HALF, HALF)]
                if step < RING - 2:
                    start(reduce_copy(m, d, step + 1, slot))
        if step < RING // 2:
            for m in range(2):
                gather_wait(0, xs, xd, m, step)
                if step < RING // 2 - 1:
                    gather_start(0, xs, xd, m, step + 1)

    tokens = act.shape[0] * RING

    def total(m):
        return jnp.concatenate([rb[m, 0, RING - 2], rb[m, 1, RING - 2]], axis=0) * (1.0 / tokens)

    encode(total(1), qb, qd)
    qd[...] = jnp.where(s > 0, qd[...], 0.0)
    hops = [
        pltpu.make_async_remote_copy(
            src_ref=source, dst_ref=target, send_sem=hop_sem.at[0, i], recv_sem=hop_sem.at[1, i],
            device_id={"section": before}, device_id_type=MESH,
        )
        for i, (source, target) in enumerate(((qb, fs.at[1, z]), (qd, fd.at[1, z])))
    ]
    for copy in hops:
        start(copy)
    encode(total(0), fs.at[0, z], fd.at[0, z])
    gather_start(1, fs, fd, 0, 0)
    for copy in hops:
        copy.wait_recv()
    gather_start(1, fs, fd, 1, 0)
    for step in range(RING // 2):
        for m in range(2):
            gather_wait(1, fs, fd, m, step)
            if step < RING // 2 - 1:
                gather_start(1, fs, fd, m, step + 1)
    for copy in sent:
        copy.wait_send()


def exchange(act, grad, warm):
    tokens, width = act.shape
    code = jax.ShapeDtypeStruct((2, RING, ROWS, WIDE), jnp.int16)
    side = jax.ShapeDtypeStruct((2, RING, 8, ROWS), jnp.float32)
    whole = pl.BlockSpec(memory_space=pltpu.VMEM)
    return pl.pallas_call(
        exchange_kernel,
        out_shape=(code, side, code, side),
        in_specs=[pl.BlockSpec(memory_space=pl.ANY), pl.BlockSpec(memory_space=pl.ANY), whole],
        out_specs=(whole,) * 4,
        scratch_shapes=[
            pltpu.VMEM((2, tokens, width + WIDE - ROWS), jnp.bfloat16),
            pltpu.VMEM((2, RING, ROWS, WIDE), jnp.float32),
            pltpu.VMEM((2, 2, RING - 1, HALF, WIDE), jnp.float32),
            pltpu.VMEM((ROWS, WIDE), jnp.int16),
            pltpu.VMEM((8, ROWS), jnp.float32),
            pltpu.SemaphoreType.DMA((2, 2)),
            pltpu.SemaphoreType.DMA((2, 2, RING - 1)),
            pltpu.SemaphoreType.DMA((2, 2, RING - 1)),
            pltpu.SemaphoreType.DMA((2, 2, 2, RING // 2, 2)),
            pltpu.SemaphoreType.DMA((2, 2, 2, RING // 2, 2)),
            pltpu.SemaphoreType.DMA((2, 2)),
        ],
        compiler_params=pltpu.CompilerParams(collective_id=0, has_side_effects=True, vmem_limit_bytes=60 << 20),
        name="exchange",
    )(act, grad, warm)


def split(value):
    high = value.astype(jnp.bfloat16)
    return high, (value - high.astype(jnp.float32)).astype(jnp.bfloat16)


def decode(code_ref, side_ref, shift, high_ref, low_ref):
    mask = diagonal_mask()

    @pl.loop(0, RING)
    def _(o):
        side = side_ref[o]
        diagonal = side[STRIP:STRIP + 1]
        root = jnp.sqrt(jnp.maximum(jnp.sum(jnp.where(mask, diagonal, 0.0), axis=1, keepdims=True), TINY))
        rows = pl.ds(pl.multiple_of(o * ROWS, ROWS), ROWS)
        for b in range(STRIP):
            block = code_ref[o, :, pl.ds(b * ROWS, ROWS)].astype(jnp.int32).astype(jnp.float32)
            block = block * side[b:b + 1] * root
            if b == 0:
                block = jnp.where(mask, diagonal + shift, block)
            high, low = split(block)
            columns = pl.ds(pl.multiple_of(lax.rem(o + b, RING) * ROWS, ROWS), ROWS)
            high_ref[rows, columns] = high
            low_ref[rows, columns] = low
            if 0 < b < STRIP - 1:
                high_ref[columns, rows] = high.T
                low_ref[columns, rows] = low.T


def refine_kernel(damping, counts, warm, fs, fd, xs, xd, out, fh, fl, xh, xl, ys, ts, y):
    m = pl.program_id(0)
    decode(xs.at[0], xd.at[0], 0.0, xh, xl)
    decode(fs.at[0], fd.at[0], damping[m], fh, fl)
    width = y.shape[1]
    tile = 256

    def put(ref, columns, value):
        high, low = split(value)
        ref[pl.ds(0, ROWS), columns] = high
        ref[pl.ds(ROWS, ROWS), columns] = low

    def product(left, high_ref, low_ref, columns):
        both = jnp.dot(left[...], high_ref[:, columns], preferred_element_type=jnp.float32)
        cross = jnp.dot(left[pl.ds(0, ROWS)], low_ref[:, columns], preferred_element_type=jnp.float32)
        return both[:ROWS] + (both[ROWS:] + cross)

    out[0] = warm[0]
    y[...] = warm[0]
    put(ys, pl.ds(0, width), warm[0])
    for index in range(ITERS):
        @pl.loop(0, 2 ** index)
        def _(_i):
            @pl.loop(0, width // tile)
            def _(j):
                columns = pl.ds(pl.multiple_of(j * tile, tile), tile)
                put(ts, columns, product(ys, fh, fl, columns))

            @pl.loop(0, width // tile)
            def _(j):
                columns = pl.ds(pl.multiple_of(j * tile, tile), tile)
                y[:, columns] = y[:, columns] - product(ts, xh, xl, columns)

            put(ys, pl.ds(0, width), y[...])

        advanced = out[0] + y[...]
        out[0] = jnp.where(index < counts[m], advanced, out[0])
        if index < ITERS - 1:
            y[...] = out[0]
            put(ys, pl.ds(0, width), out[0])


def refine(damping, counts, warm, fs, fd, xs, xd):
    width = warm.shape[2]
    scalar = pl.BlockSpec(memory_space=pltpu.SMEM)
    rows = pl.BlockSpec((1, ROWS, width), lambda m: (m, 0, 0))
    code = pl.BlockSpec((1, RING, ROWS, WIDE), lambda m: (m, 0, 0, 0))
    side = pl.BlockSpec((1, RING, 8, ROWS), lambda m: (m, 0, 0, 0))
    full = pltpu.VMEM((width, width), jnp.bfloat16)
    return pl.pallas_call(
        refine_kernel,
        grid=(2,),
        out_shape=jax.ShapeDtypeStruct(warm.shape, jnp.float32),
        in_specs=[scalar, scalar, rows, code, side, code, side],
        out_specs=rows,
        scratch_shapes=[full] * 4 + [pltpu.VMEM((2 * ROWS, width), jnp.bfloat16)] * 2 + [pltpu.VMEM((ROWS, width), jnp.float32)],
        compiler_params=pltpu.CompilerParams(vmem_limit_bytes=60 << 20),
        name="refine",
    )(damping, counts, warm, fs, fd, xs, xd)


def local(activations, sent_grads, damping, bubble_steps, warm):
    rows = warm[0, :, 0]
    codes = exchange(activations[0], sent_grads[0], rows)
    return refine(damping[0, :, 0], bubble_steps[0, :, 0], rows, *codes)[None, :, None]


def solution(mesh):
    placed = (
        P("section", "dp", "tensor"),
        P("section", "dp", "tensor"),
        P("section", None, "tensor"),
        P("section", None, "tensor"),
        P("section", None, "tensor", "dp", None),
    )
    return jax.shard_map(
        local,
        mesh=mesh,
        in_specs=placed,
        out_specs=P("section", None, "tensor", "dp", None),
        check_vma=False,
    )
```

time: 579 us -> 176 us (0.30)
  waiting for transfers between devices: 464 us -> 0 us
  Pallas kernels: 0 us -> 173 us
  matrix products: 84.6 us -> 0 us
  between operations: 17.8 us -> 0.01 us
    all_gather x6 -> x0, waiting for transfers between devices: 255 us -> none  [newton_step(): lax.all_gather(part, 'dp', axis=0, tiled=True)]
    psum x1 -> x0, waiting for transfers between devices: 207 us -> none  [local(): first_sum, second_sum = lax.psum((first_part, second_part), 'dp')]
    pallas_call x0 -> x2, Pallas kernels: none -> 173 us  [the longest x1 115 us: exchange(): pl.pallas_call(exchange_kernel, out_shape=(code, side, code, side), in_sp...]
    dot_general x14 -> x0, matrix products: 84.6 us -> none  [the longest x6 43.1 us: newton_step(): jnp.dot(x, f, precision=lax.Precision.HIGHEST)]
  transfers between devices with their start and end apart: 8 -> 0, of which waited for: 8 -> 0; matrix products, arithmetic and copies ran while one was open for 14% -> 0% of each run, Pallas kernels for 0% -> 0%
where the time goes in v1:
time: 176 us; the launch traced here: 173 us
  Pallas kernels  173 us (98%)
    pallas_call x1, Pallas kernels, exchange(): pl.pallas_call(exchange_kernel, out_shape=(code, side, code, side), in_sp...  115 us
    pallas_call x1, Pallas kernels, refine(): pl.pallas_call(refine_kernel, grid=(2,), out_shape=jax.ShapeDtypeStruct(w...  58 us

profile of v1, /device:TPU:16, one launch (start us, length us, event | category | flops | bytes accessed | tf_op | source)
XLA Modules:
  0.0 173.4 jit_solution(6361119355805150486)
XLA Ops:
  0.0 115.4 %exchange.1 = (s16[2,8,128,640]{3,2,1,0:T(8,128)(2,1)}, f32[2,8,8,128]{3,2,1,0:T(8,128)}, s16[2,8,128,640]{3,2,1,0:T(8,128)(2,1)}, f32[2,8,8,128]{3,2,1,0:T(8,128)}) custom-call(bf16[1024,1024]{1,0:T(8,128)(2,1)} %bitcast.10, bf16[1024,1024]{1,0:T(8,128)(2,1)} %bitcast.11, f32[2,128,1024]{2,1,0:T(8,128)} %bitcast.8), custom_call_target="tpu_custom_call" | custom-call | tf_op jit(solution)/shard_map/exchange/pallas_call | solution.py:186
  115.4 58.0 %refine.1 = f32[2,128,1024]{2,1,0:T(8,128)} custom-call(f32[2]{0:T(128)} %bitcast.12, s32[2]{0:T(128)} %bitcast.13, f32[2,128,1024]{2,1,0:T(8,128)} %bitcast.9, s16[2,8,128,640]{3,2,1,0:T(8,128)(2,1)} %get-tuple-element.9.fs, f32[2,8,8,128]{3,2,1,0:T(8,128)} %get-tuple-element.10.fd, s16[2,8,128,640]{3,2,1,0:T(8,128)(2,1)} %get-tuple-element.11.xs, ...), custom_call_target="tpu_custom_call" | custom-call | tf_op jit(solution)/shard_map/refine/pallas_call | solution.py:286

commit v2 on v0

v2 whole, which is shorter than its diff:
```python
import functools

import jax
import jax.numpy as jnp
from jax import lax
from jax.experimental import pallas as pl
from jax.experimental.pallas import tpu as pltpu
from jax.sharding import PartitionSpec as P

MESH = pl.DeviceIdType.MESH
ITERS = 3
RING = 8
ROWS = 128
STRIP = 5
WIDE = STRIP * ROWS
HALF = ROWS // 2
LEVELS = 32767.0
TINY = 1e-30


def diagonal_mask(rows, first):
    row = lax.broadcasted_iota(jnp.int32, (rows, ROWS), 0) + first
    column = lax.broadcasted_iota(jnp.int32, (rows, ROWS), 1)
    return row == column


def encode(strip, code_ref, side_ref, first=0):
    mask = diagonal_mask(strip.shape[0], first)
    square = strip[:, :ROWS]
    diagonal = jnp.where(mask, square, 0.0)
    along_lanes = jnp.sum(diagonal, axis=0, keepdims=True)
    along_rows = jnp.sum(diagonal, axis=1, keepdims=True)
    rest = jnp.concatenate([jnp.where(mask, 0.0, square), strip[:, ROWS:]], axis=1)
    scaled = rest / jnp.sqrt(jnp.maximum(along_rows, TINY))
    largest = jnp.maximum(jnp.max(jnp.abs(scaled), axis=0, keepdims=True), TINY)
    code_ref[...] = jnp.round(scaled * (LEVELS / largest)).astype(jnp.int32).astype(jnp.int16)
    largest = largest / LEVELS
    pieces = [largest[:, b * ROWS:(b + 1) * ROWS] for b in range(STRIP)]
    zero = jnp.zeros_like(along_lanes)
    side_ref[...] = jnp.concatenate(pieces + [along_lanes, zero, zero], axis=0)


def decode(code, side, first=0, shift=0.0):
    rows = code.shape[0]
    mask = diagonal_mask(rows, first)
    diagonal = side[STRIP:STRIP + 1]
    root = jnp.sqrt(jnp.maximum(jnp.sum(jnp.where(mask, diagonal, 0.0), axis=1, keepdims=True), TINY))
    blocks = []
    for b in range(STRIP):
        block = code[:, b * ROWS:(b + 1) * ROWS].astype(jnp.int32).astype(jnp.float32) * side[b:b + 1] * root
        if b == 0:
            block = jnp.where(mask, diagonal + shift, block)
        blocks.append(block)
    return blocks


def split(value):
    high = value.astype(jnp.bfloat16)
    return high, (value - high.astype(jnp.float32)).astype(jnp.bfloat16)


def kernel(
    damping, counts, act, grad, warm, out,
    a, g, rb, rside, xs, xd, fs, fd, qb, qd, full, ys, ts, y,
    in_sem, rs_send, rs_recv, ag_send, ag_recv, hop_sem,
):
    z = lax.axis_index("dp")
    s = lax.axis_index("section")
    sections = lax.axis_size("section")
    right, left = lax.rem(z + 1, RING), lax.rem(z + RING - 1, RING)
    before, behind = lax.rem(s + sections - 1, sections), lax.rem(s + 1, sections)
    width = act.shape[1]
    extra = WIDE - ROWS
    tokens = act.shape[0] * RING
    last_step = RING // 2 - 1
    last_hop = RING - 2
    sent = []

    def start(copies):
        for copy in copies:
            copy.start()
            sent.append(copy)

    def remote(source, target, send, receive, device):
        return pltpu.make_async_remote_copy(
            src_ref=source, dst_ref=target, send_sem=send, recv_sem=receive, device_id=device, device_id_type=MESH,
        )

    def owner_of(d, distance):
        return lax.rem(z + (RING - distance, distance)[d], RING)

    def half(d):
        return pl.ds(d * HALF, HALF)

    def gram(m, owner):
        first = pl.multiple_of(owner * ROWS, ROWS)
        g[m, owner] = lax.dot_general(
            a[m, :, pl.ds(first, ROWS)], a[m, :, pl.ds(first, WIDE)],
            (((0,), (0,)), ((), ())), preferred_element_type=jnp.float32,
        )

    def reduce_copies(m, d, hop, source):
        device = {"dp": (right, left)[d]}
        return [
            remote(ref.at[m, d, source], ref.at[m, d, hop], rs_send.at[m, d, hop, i], rs_recv.at[m, d, hop, i], device)
            for i, ref in enumerate((rb, rside))
        ]

    def reduce_first(m):
        for d in range(2):
            owner = owner_of(d, 1)
            gram(m, owner)
            encode(g[m, owner, half(d)], rb.at[m, d, RING - 1], rside.at[m, d, RING - 1], d * HALF)

    def reduce_start(m):
        for d in range(2):
            start(reduce_copies(m, d, 0, RING - 1))

    def gram_rest(m):
        @pl.loop(0, RING - 2)
        def _(j):
            gram(m, lax.rem(z + 2 + j + j // (RING - 3), RING))

    def reduce_hop(m, hop):
        for d in range(2):
            for copy in reduce_copies(m, d, hop, hop):
                copy.wait_recv()
            owner = owner_of(d, (hop + 2) % RING)
            received = jnp.concatenate(decode(rb[m, d, hop], rside[m, d, hop], d * HALF), axis=1)
            value = received + g[m, owner, half(d)]
            if hop < last_hop:
                encode(value, rb.at[m, d, hop], rside.at[m, d, hop], d * HALF)
                start(reduce_copies(m, d, hop + 1, hop))
            else:
                g[m, owner, half(d)] = value * (1.0 / tokens)

    stores = ((xs, xd), (fs, fd))

    def gather_copies(which, m, d, step, owner):
        codes, sides = stores[which]
        rows = half(d) if step == last_step else pl.ds(0, ROWS)
        pairs = [codes.at[m, owner, rows]]
        if step < last_step or d == 0:
            pairs.append(sides.at[m, owner])
        return [
            remote(ref, ref, ag_send.at[which, m, d, step, i], ag_recv.at[which, m, d, step, i], {"dp": (right, left)[d]})
            for i, ref in enumerate(pairs)
        ]

    def gather_start(which, m, step):
        for d in range(2):
            start(gather_copies(which, m, d, step, owner_of(d, step)))

    def gather_step(which, m, step):
        for d in range(2):
            for copy in gather_copies(which, m, d, step, owner_of(d, step + 1)):
                copy.wait_recv()
        if step < last_step:
            gather_start(which, m, step + 1)

    def spread(which, m, owner):
        codes, sides = stores[which]
        shift = (0.0, damping[m])[which]
        high_ref, low_ref = full.at[which, m, 0], full.at[which, m, 1]
        rows = pl.ds(pl.multiple_of(owner * ROWS, ROWS), ROWS)
        for b, block in enumerate(decode(codes[m, owner], sides[m, owner], 0, shift)):
            high, low = split(block)
            columns = pl.ds(pl.multiple_of(lax.rem(owner + b, RING) * ROWS, ROWS), ROWS)
            high_ref[rows, columns] = high
            low_ref[rows, columns] = low
            if 0 < b < STRIP - 1:
                high_ref[columns, rows] = high.T
                low_ref[columns, rows] = low.T

    def spread_step(which, m, step):
        if step == last_step:
            spread(which, m, owner_of(1, step + 1))
        else:
            @pl.loop(0, 2)
            def _(d):
                spread(which, m, lax.rem(z + RING + (2 * d - 1) * (step + 1), RING))

    tile = 512

    def put(ref, columns, value):
        high, low = split(value)
        ref[pl.ds(0, ROWS), columns] = high
        ref[pl.ds(ROWS, ROWS), columns] = low

    def product(rows, which, m, columns):
        both = jnp.dot(rows[...], full[which, m, 0, :, columns], preferred_element_type=jnp.float32)
        cross = jnp.dot(rows[pl.ds(0, ROWS)], full[which, m, 1, :, columns], preferred_element_type=jnp.float32)
        return both[:ROWS] + (both[ROWS:] + cross)

    def begin(m):
        out[m] = warm[m]
        y[...] = warm[m]
        put(ys, pl.ds(0, width), warm[m])

    def by_factor(m):
        @pl.loop(0, width // tile)
        def _(j):
            columns = pl.ds(pl.multiple_of(j * tile, tile), tile)
            put(ts, columns, product(ys, 1, m, columns))

    def by_inverse(m, index, last):
        @pl.loop(0, width // tile)
        def _(j):
            columns = pl.ds(pl.multiple_of(j * tile, tile), tile)
            value = y[:, columns] - product(ts, 0, m, columns)
            if last:
                old = out[m, :, columns]
                value = jnp.where(index < counts[m], old + value, old)
                out[m, :, columns] = value
            y[:, columns] = value
            put(ys, columns, value)

    loads = []
    for m, source in enumerate((act, grad)):
        loads.append((
            pltpu.make_async_copy(source, a.at[m, :, pl.ds(0, width)], in_sem.at[m, 0]),
            pltpu.make_async_copy(source.at[:, pl.ds(0, extra)], a.at[m, :, pl.ds(width, extra)], in_sem.at[m, 1]),
        ))
        for copy in loads[-1]:
            copy.start()

    barrier = pltpu.get_barrier_semaphore()
    for target in ({"dp": right}, {"dp": left}, {"section": before}, {"section": behind}):
        pl.semaphore_signal(barrier, inc=1, device_id=target, device_id_type=MESH)

    for m in range(2):
        blocks = [
            warm[m, :, pl.ds(pl.multiple_of(lax.rem(z + b, RING) * ROWS, ROWS), ROWS)] for b in range(STRIP)
        ]
        encode(jnp.concatenate(blocks, axis=1), xs.at[m, z], xd.at[m, z])

    for copy in loads[0]:
        copy.wait()
    reduce_first(0)
    pl.semaphore_wait(barrier, 4)
    reduce_start(0)
    gather_start(0, 0, 0)
    gram_rest(0)
    for copy in loads[1]:
        copy.wait()
    reduce_first(1)
    gram_rest(1)

    for hop in range(last_hop + 1):
        reduce_hop(0, hop)
        if hop <= last_step:
            gather_step(0, 0, hop)
        if hop == 2:
            reduce_start(1)
        if hop == last_hop:
            encode(g[0, z], fs.at[0, z], fd.at[0, z])
            gather_start(1, 0, 0)
        if hop >= 3:
            reduce_hop(1, hop - 3)
        if hop == 3:
            spread(0, 0, z)
        elif hop > 3:
            spread_step(0, 0, hop - 4)

    hops = [
        remote(source, target, hop_sem.at[0, i], hop_sem.at[1, i], {"section": before})
        for i, (source, target) in enumerate(((qb, fs.at[1, z]), (qd, fd.at[1, z])))
    ]
    spread(1, 0, z)
    spread_step(0, 0, last_step)
    for step in range(last_step + 1):
        gather_step(1, 0, step)
        if step < last_step:
            reduce_hop(1, step + last_hop - 2)
        if step == last_step - 1:
            encode(g[1, z], qb, qd)
            qd[...] = jnp.where(s > 0, qd[...], 0.0)
            start(hops)
            gather_start(0, 1, 0)
        spread_step(1, 0, step)

    def arrive():
        for copy in hops:
            copy.wait_recv()
        gather_start(1, 1, 0)
        spread(0, 1, z)
        spread(1, 1, z)

    def advance(which, step):
        gather_step(which, 1, step)
        spread_step(which, 1, step)

    events = [None, arrive]
    for step in range(last_step + 1):
        events += [functools.partial(advance, 0, step), None, functools.partial(advance, 1, step)]
    events = iter(events)

    def event():
        do = next(events, None)
        if do is not None:
            do()

    begin(0)
    for index in range(ITERS):
        for i in range(2 ** index):
            by_factor(0)
            event()
            by_inverse(0, index, i == 2 ** index - 1)
            event()
    for do in events:
        if do is not None:
            do()

    begin(1)
    for index in range(ITERS):
        if index:
            @pl.loop(0, 2 ** index - 1)
            def _(_i):
                by_factor(1)
                by_inverse(1, index, False)
        by_factor(1)
        by_inverse(1, index, True)

    for copy in sent:
        copy.wait_send()


def run(damping, counts, act, grad, warm):
    tokens, width = act.shape
    whole = pl.BlockSpec(memory_space=pltpu.VMEM)
    scalar = pl.BlockSpec(memory_space=pltpu.SMEM)
    code = pltpu.VMEM((2, RING, ROWS, WIDE), jnp.int16)
    side = pltpu.VMEM((2, RING, 8, ROWS), jnp.float32)
    return pl.pallas_call(
        kernel,
        out_shape=jax.ShapeDtypeStruct(warm.shape, jnp.float32),
        in_specs=[scalar, scalar, pl.BlockSpec(memory_space=pl.ANY), pl.BlockSpec(memory_space=pl.ANY), whole],
        out_specs=whole,
        scratch_shapes=[
            pltpu.VMEM((2, tokens, width + WIDE - ROWS), jnp.bfloat16),
            pltpu.VMEM((2, RING, ROWS, WIDE), jnp.float32),
            pltpu.VMEM((2, 2, RING, HALF, WIDE), jnp.int16),
            pltpu.VMEM((2, 2, RING, 8, ROWS), jnp.float32),
            code, side, code, side,
            pltpu.VMEM((ROWS, WIDE), jnp.int16),
            pltpu.VMEM((8, ROWS), jnp.float32),
            pltpu.VMEM((2, 2, 2, width, width), jnp.bfloat16),
            pltpu.VMEM((2 * ROWS, width), jnp.bfloat16),
            pltpu.VMEM((2 * ROWS, width), jnp.bfloat16),
            pltpu.VMEM((ROWS, width), jnp.float32),
            pltpu.SemaphoreType.DMA((2, 2)),
            pltpu.SemaphoreType.DMA((2, 2, RING - 1, 2)),
            pltpu.SemaphoreType.DMA((2, 2, RING - 1, 2)),
            pltpu.SemaphoreType.DMA((2, 2, 2, RING // 2, 2)),
            pltpu.SemaphoreType.DMA((2, 2, 2, RING // 2, 2)),
            pltpu.SemaphoreType.DMA((2, 2)),
        ],
        compiler_params=pltpu.CompilerParams(collective_id=0, has_side_effects=True, vmem_limit_bytes=62 << 20),
        name="factors",
    )(damping, counts, act, grad, warm)


def local(activations, sent_grads, damping, bubble_steps, warm):
    refined = run(damping[0, :, 0], bubble_steps[0, :, 0], activations[0], sent_grads[0], warm[0, :, 0])
    return refined[None, :, None]


def solution(mesh):
    placed = (
        P("section", "dp", "tensor"),
        P("section", "dp", "tensor"),
        P("section", None, "tensor"),
        P("section", None, "tensor"),
        P("section", None, "tensor", "dp", None),
    )
    return jax.shard_map(
        local,
        mesh=mesh,
        in_specs=placed,
        out_specs=P("section", None, "tensor", "dp", None),
        check_vma=False,
    )
```

time: 579 us -> 122 us (0.21)
  waiting for transfers between devices: 464 us -> 0 us
  Pallas kernels: 0 us -> 119 us
  matrix products: 84.6 us -> 0 us
  between operations: 17.8 us -> 0.01 us
    all_gather x6 -> x0, waiting for transfers between devices: 255 us -> none  [newton_step(): lax.all_gather(part, 'dp', axis=0, tiled=True)]
    psum x1 -> x0, waiting for transfers between devices: 207 us -> none  [local(): first_sum, second_sum = lax.psum((first_part, second_part), 'dp')]
    pallas_call x0 -> x1, Pallas kernels: none -> 119 us  [run(): pl.pallas_call(kernel, out_shape=jax.ShapeDtypeStruct(warm.shape, jnp.flo...]
    dot_general x14 -> x0, matrix products: 84.6 us -> none  [the longest x6 43.1 us: newton_step(): jnp.dot(x, f, precision=lax.Precision.HIGHEST)]
  transfers between devices with their start and end apart: 8 -> 0, of which waited for: 8 -> 0; matrix products, arithmetic and copies ran while one was open for 14% -> 0% of each run, Pallas kernels for 0% -> 0%
where the time goes in v2:
time: 122 us; the launch traced here: 121 us
  Pallas kernels  119 us (98%)
  local copies, waits for them, and re-layouts  2.31 us (2%)
    pallas_call x1, Pallas kernels, run(): pl.pallas_call(kernel, out_shape=jax.ShapeDtypeStruct(warm.shape, jnp.flo...  119 us

profile of v2, /device:TPU:16, one launch (start us, length us, event | category | flops | bytes accessed | tf_op | source)
XLA Modules:
  0.0 121.5 jit_solution(13611361835221701231)
XLA Ops:
  0.0 119.2 %factors.1 = f32[2,128,1024]{2,1,0:T(8,128)} custom-call(f32[2]{0:T(128)} %bitcast.12, s32[2]{0:T(128)} %bitcast.13, bf16[1024,1024]{1,0:T(8,128)(2,1)} %bitcast.9, bf16[1024,1024]{1,0:T(8,128)(2,1)} %bitcast.10, f32[2,128,1024]{2,1,0:T(8,128)} %bitcast.11), custom_call_target="tpu_custom_call" | custom-call | tf_op jit(solution)/shard_map/factors/pallas_call | solution.py:334
  119.2 2.3 %copy.8 = f32[1,2,1,128,1024]{4,3,2,1,0:T(8,128)} copy(f32[1,2,1,128,1024]{4,3,2,1,0:T(8,128)} %bitcast.8) | data formatting | bytes 2097152

commit v3 on v2

v3 whole, which is shorter than its diff:
```python
import functools

import jax
import jax.numpy as jnp
from jax import lax
from jax.experimental import pallas as pl
from jax.experimental.pallas import tpu as pltpu
from jax.sharding import PartitionSpec as P

MESH = pl.DeviceIdType.MESH
ITERS = 3
RING = 8
ROWS = 128
STRIP = 5
WIDE = STRIP * ROWS
HALF = ROWS // 2
LEVELS = 32767.0
TINY = 1e-30


def diagonal_mask(rows, first):
    row = lax.broadcasted_iota(jnp.int32, (rows, ROWS), 0) + first
    column = lax.broadcasted_iota(jnp.int32, (rows, ROWS), 1)
    return row == column


def encode(strip, code_ref, side_ref, h):
    mask = diagonal_mask(HALF, h * HALF)
    square = strip[:, :ROWS]
    diagonal = jnp.where(mask, square, 0.0)
    along_lanes = jnp.sum(diagonal, axis=0, keepdims=True)
    along_rows = jnp.sum(diagonal, axis=1, keepdims=True)
    rest = jnp.concatenate([jnp.where(mask, 0.0, square), strip[:, ROWS:]], axis=1)
    scaled = rest * (1.0 / jnp.sqrt(jnp.maximum(along_rows, TINY)))
    largest = jnp.maximum(jnp.max(jnp.abs(scaled), axis=0, keepdims=True), TINY)
    code_ref[...] = jnp.round(scaled * (LEVELS / largest)).astype(jnp.int32).astype(jnp.int16)
    largest = largest / LEVELS
    pieces = [largest[:, b * ROWS:(b + 1) * ROWS] for b in range(STRIP - h)]
    zero = jnp.zeros_like(along_lanes)
    side_ref[...] = jnp.concatenate(pieces + [zero] * h + [along_lanes, zero, zero], axis=0)


def decode(code, side, h, shift=0.0):
    mask = diagonal_mask(HALF, h * HALF)
    diagonal = side[STRIP:STRIP + 1]
    root = jnp.sqrt(jnp.maximum(jnp.sum(jnp.where(mask, diagonal, 0.0), axis=1, keepdims=True), TINY))
    blocks = []
    for b in range(STRIP - h):
        block = code[:, b * ROWS:(b + 1) * ROWS].astype(jnp.int32).astype(jnp.float32) * side[b:b + 1] * root
        if b == 0:
            block = jnp.where(mask, diagonal + shift, block)
        blocks.append(block)
    return blocks


def left_lanes():
    return lax.broadcasted_iota(jnp.int32, (HALF, ROWS), 1) < HALF


def halves(strip):
    lower = strip[HALF:]
    corner = pltpu.roll(lower[:, WIDE - ROWS:], HALF, 1)
    corners = jnp.where(left_lanes(), corner, lower[:, :ROWS])
    return strip[:HALF], jnp.concatenate([corners, lower[:, ROWS:WIDE - ROWS]], axis=1)


def split(value):
    high = value.astype(jnp.bfloat16)
    return high, (value - high.astype(jnp.float32)).astype(jnp.bfloat16)


def kernel(
    damping, counts, act, grad, warm, out,
    a, g0, g1, r0, r1, rside, x0, x1, xd, f0, f1, fd, q0, q1, qd, full, ys, ts, y,
    in_sem, rs_send, rs_recv, ag_send, ag_recv, hop_sem,
):
    z = lax.axis_index("dp")
    s = lax.axis_index("section")
    sections = lax.axis_size("section")
    right, left = lax.rem(z + 1, RING), lax.rem(z + RING - 1, RING)
    before, behind = lax.rem(s + sections - 1, sections), lax.rem(s + 1, sections)
    width = act.shape[1]
    extra = WIDE - ROWS
    tokens = act.shape[0] * RING
    last_step = RING // 2 - 1
    last_hop = RING - 2
    early = 0
    sent = []

    def start(copies):
        for copy in copies:
            copy.start()
            sent.append(copy)

    def remote(source, target, send, receive, device):
        return pltpu.make_async_remote_copy(
            src_ref=source, dst_ref=target, send_sem=send, recv_sem=receive, device_id=device, device_id_type=MESH,
        )

    def owner_of(d, distance):
        return lax.rem(z + (RING - distance, distance)[d], RING)

    g, rb, xs, fs, qb = (g0, g1), (r0, r1), (x0, x1), (f0, f1), (q0, q1)

    def gram(m, owner):
        first = pl.multiple_of(owner * ROWS, ROWS)
        strip = lax.dot_general(
            a[m, :, pl.ds(first, ROWS)], a[m, :, pl.ds(first, WIDE)],
            (((0,), (0,)), ((), ())), preferred_element_type=jnp.float32,
        )
        for h, value in enumerate(halves(strip)):
            g[h][m, owner] = value

    def reduce_copies(m, d, hop, source):
        device = {"dp": (right, left)[d]}
        pairs = ((rb[d ^ m].at[m, source], rb[d ^ m].at[m, hop]), (rside.at[m, d, source], rside.at[m, d, hop]))
        return [
            remote(a_ref, b_ref, rs_send.at[m, d, hop, i], rs_recv.at[m, d, hop, i], device)
            for i, (a_ref, b_ref) in enumerate(pairs)
        ]

    def reduce_start(m):
        for d in range(2):
            start(reduce_copies(m, d, 0, RING - 1))

    def reduce_hop(m, hop):
        for d in range(2):
            h = d ^ m
            for copy in reduce_copies(m, d, hop, hop):
                copy.wait_recv()
            owner = owner_of(d, (hop + 2) % RING)
            received = jnp.concatenate(decode(rb[h][m, hop], rside[m, d, hop], h), axis=1)
            value = received + g[h][m, owner]
            if hop < last_hop:
                encode(value, rb[h].at[m, hop], rside.at[m, d, hop], h)
                start(reduce_copies(m, d, hop + 1, hop))
            else:
                g[h][m, owner] = value * (1.0 / tokens)

    stores = ((xs, xd), (fs, fd))

    def gather_copies(which, m, d, step, h, owner):
        codes, sides = stores[which]
        return [
            remote(ref, ref, ag_send.at[which, m, d, step, h, i], ag_recv.at[which, m, d, step, h, i], {"dp": (right, left)[d]})
            for i, ref in enumerate((codes[h].at[m, owner], sides.at[m, h, owner]))
        ]

    def gather_start(which, m):
        for h in range(2):
            for d in range(2):
                start(gather_copies(which, m, d, 0, h ^ d, owner_of(d, 0)))

    def gather_turn(which, m, count):
        step, turn = count // 2, count % 2
        for d in range(2):
            h = turn ^ d
            owner = owner_of(d, step + 1)
            for copy in gather_copies(which, m, d, step, h, owner):
                copy.wait_recv()
            if step + 1 + turn <= last_step:
                start(gather_copies(which, m, d, step + 1, h, owner))

    def spread(which, m, owner):
        codes, sides = stores[which]
        shift = (0.0, damping[m])[which]
        upper, lower = (decode(codes[h][m, owner], sides[m, h, owner], h, shift) for h in range(2))
        far = lax.rem(owner + STRIP - 1, RING)
        left = left_lanes()
        empty = jnp.zeros((HALF, ROWS), jnp.float32)

        def store(block, row_block, column_block, bottom):
            columns = pl.ds(pl.multiple_of(column_block * ROWS, ROWS), ROWS)
            rows = pl.ds(pl.multiple_of(row_block * ROWS + bottom * HALF, HALF), block.shape[0])
            for i, part in enumerate(split(block)):
                full[which, m, i, rows, columns] = part

        def merge(block, row_block, column_block, mask):
            columns = pl.ds(pl.multiple_of(column_block * ROWS, ROWS), ROWS)
            rows = pl.ds(pl.multiple_of(row_block * ROWS + HALF, HALF), HALF)
            for i, part in enumerate(split(block)):
                old = full[which, m, i, rows, columns].astype(jnp.float32)
                full[which, m, i, rows, columns] = jnp.where(mask, part.astype(jnp.float32), old).astype(jnp.bfloat16)

        flipped = jnp.concatenate([upper[0], empty], axis=0).T
        store(jnp.concatenate([upper[0], jnp.where(left, flipped[HALF:], lower[0])], axis=0), owner, owner, 0)
        for b in range(1, STRIP - 1):
            block = jnp.concatenate([upper[b], lower[b]], axis=0)
            other = lax.rem(owner + b, RING)
            store(block, owner, other, 0)
            store(block.T, other, owner, 0)
        store(upper[STRIP - 1], owner, far, 0)
        merge(pltpu.roll(lower[0], HALF, 1), owner, far, jnp.logical_not(left))
        merge(jnp.concatenate([upper[STRIP - 1], empty], axis=0).T[HALF:], far, owner, left)

    def spread_step(which, m, step):
        if step == last_step:
            spread(which, m, owner_of(1, step + 1))
        else:
            @pl.loop(0, 2)
            def _(d):
                spread(which, m, lax.rem(z + RING + (2 * d - 1) * (step + 1), RING))

    tile = 512

    def put(ref, columns, value):
        high, low = split(value)
        ref[pl.ds(0, ROWS), columns] = high
        ref[pl.ds(ROWS, ROWS), columns] = low

    def product(rows, which, m, columns):
        both = jnp.dot(rows[...], full[which, m, 0, :, columns], preferred_element_type=jnp.float32)
        cross = jnp.dot(rows[pl.ds(0, ROWS)], full[which, m, 1, :, columns], preferred_element_type=jnp.float32)
        return both[:ROWS] + (both[ROWS:] + cross)

    def begin(m):
        out[m] = warm[m]
        y[...] = warm[m]
        put(ys, pl.ds(0, width), warm[m])

    def by_factor(m):
        @pl.loop(0, width // tile)
        def _(j):
            columns = pl.ds(pl.multiple_of(j * tile, tile), tile)
            put(ts, columns, product(ys, 1, m, columns))

    def by_inverse(m, index, last):
        @pl.loop(0, width // tile)
        def _(j):
            columns = pl.ds(pl.multiple_of(j * tile, tile), tile)
            value = y[:, columns] - product(ts, 0, m, columns)
            if last:
                old = out[m, :, columns]
                value = jnp.where(index < counts[m], old + value, old)
                out[m, :, columns] = value * 0.5 if index == ITERS - 1 else value
            y[:, columns] = value
            put(ys, columns, value)

    loads = []
    for m, source in enumerate((act, grad)):
        loads.append((
            pltpu.make_async_copy(source, a.at[m, :, pl.ds(0, width)], in_sem.at[m, 0]),
            pltpu.make_async_copy(source.at[:, pl.ds(0, extra)], a.at[m, :, pl.ds(width, extra)], in_sem.at[m, 1]),
        ))
        for copy in loads[-1]:
            copy.start()

    barrier = pltpu.get_barrier_semaphore()
    for target in ({"dp": right}, {"dp": left}, {"section": before}, {"section": behind}):
        pl.semaphore_signal(barrier, inc=1, device_id=target, device_id_type=MESH)

    for m in range(2):
        blocks = [
            warm[m, :, pl.ds(pl.multiple_of(lax.rem(z + b, RING) * ROWS, ROWS), ROWS)] for b in range(STRIP)
        ]
        for h, value in enumerate(halves(jnp.concatenate(blocks, axis=1))):
            encode(value, xs[h].at[m, z], xd.at[m, h, z], h)

    pl.semaphore_wait(barrier, 4)
    gather_start(0, 0)
    for m in range(2):
        for copy in loads[m]:
            copy.wait()
        for d in range(2):
            owner = owner_of(d, 1)
            gram(m, owner)
            encode(g[d ^ m][m, owner], rb[d ^ m].at[m, RING - 1], rside.at[m, d, RING - 1], d ^ m)
        reduce_start(m)

    hops = [
        remote(source, target, hop_sem.at[0, i], hop_sem.at[1, i], {"section": before})
        for i, (source, target) in enumerate((
            (q0, f0.at[1, z]), (q1, f1.at[1, z]), (qd.at[0], fd.at[1, 0, z]), (qd.at[1], fd.at[1, 1, z]),
        ))
    ]
    turns = RING - 1

    def turned(which, m, count):
        gather_turn(which, m, count)
        if count == turns - 1:
            spread_step(which, m, last_step)
        elif count % 2:
            spread_step(which, m, count // 2)

    slots = [functools.partial(turned, 0, 0, count) for count in range(turns)]
    slots += [functools.partial(gather_start, 0, 1)] + [functools.partial(turned, 0, 1, count) for count in range(early)]
    slots = iter(slots)
    for hop in range(last_hop + 1):
        for m in range(2):
            if hop < 2:
                gram(m, owner_of(0, hop + 2))
                gram(m, owner_of(1, hop + 2))
            elif hop < 4:
                gram(m, owner_of(0, (hop + 2, RING)[hop - 2]))
            reduce_hop(m, hop)
            if hop == last_hop and m == 0:
                for h in range(2):
                    encode(g[h][0, z], fs[h].at[0, z], fd.at[0, h, z], h)
                gather_start(1, 0)
            do = next(slots, None)
            if do is not None:
                do()
    for h in range(2):
        encode(g[h][1, z], qb[h], qd.at[h], h)
    qd[...] = jnp.where(s > 0, qd[...], 0.0)
    start(hops)
    for do in slots:
        do()
    spread(0, 0, z)
    spread(1, 0, z)
    for count in range(turns):
        turned(1, 0, count)
        if count == turns - 3:
            for copy in hops:
                copy.wait_recv()
            gather_start(1, 1)
    spread(0, 1, z)
    spread(1, 1, z)

    rest = [functools.partial(turned, 0, 1, count) for count in range(early, turns)]
    main = [functools.partial(turned, 1, 1, count) for count in range(turns)]
    waiting = []
    for i in range(turns):
        waiting += main[i:i + 1] + rest[i:i + 1]
    products = 2 * (2 ** ITERS - 1)
    events = [[] for _ in range(products)]
    for i, do in enumerate(waiting):
        events[(i + 1) * products // len(waiting) - 1].append(do)
    events = iter(events)

    def event():
        for do in next(events):
            do()

    begin(0)
    for index in range(ITERS):
        for i in range(2 ** index):
            by_factor(0)
            event()
            by_inverse(0, index, i == 2 ** index - 1)
            event()
    begin(1)
    for index in range(ITERS):
        if index:
            @pl.loop(0, 2 ** index - 1)
            def _(_i):
                by_factor(1)
                by_inverse(1, index, False)
        by_factor(1)
        by_inverse(1, index, True)

    for copy in sent:
        copy.wait_send()


def run(damping, counts, act, grad, warm):
    tokens, width = act.shape
    whole = pl.BlockSpec(memory_space=pltpu.VMEM)
    scalar = pl.BlockSpec(memory_space=pltpu.SMEM)
    def pair(shape, dtype):
        return [pltpu.VMEM(shape + (HALF, WIDE - h * ROWS), dtype) for h in range(2)]

    side = pltpu.VMEM((2, 2, RING, 8, ROWS), jnp.float32)
    return pl.pallas_call(
        kernel,
        out_shape=jax.ShapeDtypeStruct(warm.shape, jnp.float32),
        in_specs=[scalar, scalar, pl.BlockSpec(memory_space=pl.ANY), pl.BlockSpec(memory_space=pl.ANY), whole],
        out_specs=whole,
        scratch_shapes=[
            pltpu.VMEM((2, tokens, width + WIDE - ROWS), jnp.bfloat16),
            *pair((2, RING), jnp.float32),
            *pair((2, RING), jnp.int16),
            side,
            *pair((2, RING), jnp.int16),
            side,
            *pair((2, RING), jnp.int16),
            side,
            *pair((), jnp.int16),
            pltpu.VMEM((2, 8, ROWS), jnp.float32),
            pltpu.VMEM((2, 2, 2, width, width), jnp.bfloat16),
            pltpu.VMEM((2 * ROWS, width), jnp.bfloat16),
            pltpu.VMEM((2 * ROWS, width), jnp.bfloat16),
            pltpu.VMEM((ROWS, width), jnp.float32),
            pltpu.SemaphoreType.DMA((2, 2)),
            pltpu.SemaphoreType.DMA((2, 2, RING - 1, 2)),
            pltpu.SemaphoreType.DMA((2, 2, RING - 1, 2)),
            pltpu.SemaphoreType.DMA((2, 2, 2, RING // 2, 2, 2)),
            pltpu.SemaphoreType.DMA((2, 2, 2, RING // 2, 2, 2)),
            pltpu.SemaphoreType.DMA((2, 4)),
        ],
        compiler_params=pltpu.CompilerParams(collective_id=0, has_side_effects=True, vmem_limit_bytes=62 << 20),
        name="factors",
    )(damping, counts, act, grad, warm)


def local(activations, sent_grads, damping, bubble_steps, warm):
    refined = run(damping[0, :, 0], bubble_steps[0, :, 0], activations[0], sent_grads[0], warm[0, :, 0])
    return (2.0 * refined)[None, :, None]


def solution(mesh):
    placed = (
        P("section", "dp", "tensor"),
        P("section", "dp", "tensor"),
        P("section", None, "tensor"),
        P("section", None, "tensor"),
        P("section", None, "tensor", "dp", None),
    )
    return jax.shard_map(
        local,
        mesh=mesh,
        in_specs=placed,
        out_specs=P("section", None, "tensor", "dp", None),
        check_vma=False,
    )
```

time: 122 us -> 114 us (0.934)
  Pallas kernels: 119 us -> 110 us
  other arithmetic: 0 us -> 2.31 us
  local copies, waits for them, and re-layouts: 2.31 us -> 0 us
    pallas_call x1, Pallas kernels: 119 us -> 110 us  [run(): pl.pallas_call(kernel, out_shape=jax.ShapeDtypeStruct(warm.shape, jnp.flo...]
    broadcast_in_dim x0 -> x1, other arithmetic: none -> 2.31 us  [local(): return (2.0 * refined)[None, :, None]]
    unnamed x1 -> x0, local copies, waits for them, and re-layouts: 2.31 us -> none
where the time goes in v3:
time: 114 us; the launch traced here: 113 us
  Pallas kernels  110 us (96%)
  other arithmetic  2.31 us (2%)
    pallas_call x1, Pallas kernels, run(): pl.pallas_call(kernel, out_shape=jax.ShapeDtypeStruct(warm.shape, jnp.flo...  110 us
    broadcast_in_dim x1, other arithmetic, local(): return (2.0 * refined)[None, :, None]  2.31 us

profile of v3, /device:TPU:16, one launch (start us, length us, event | category | flops | bytes accessed | tf_op | source)
XLA Modules:
  0.0 112.8 jit_solution(6587039990020487444)
XLA Ops:
  0.0 110.5 %factors.1 = f32[2,128,1024]{2,1,0:T(8,128)} custom-call(f32[2]{0:T(128)} %bitcast.12, s32[2]{0:T(128)} %bitcast.13, bf16[1024,1024]{1,0:T(8,128)(2,1)} %bitcast.9, bf16[1024,1024]{1,0:T(8,128)(2,1)} %bitcast.10, f32[2,128,1024]{2,1,0:T(8,128)} %bitcast.11), custom_call_target="tpu_custom_call" | custom-call | tf_op jit(solution)/shard_map/factors/pallas_call | solution.py:364
  110.5 2.3 %multiply_bitcast_fusion = f32[1,2,1,128,1024]{4,3,2,1,0:T(8,128)} fusion(f32[2,128,1024]{2,1,0:T(8,128)} %factors.1), kind=kLoop, calls=%fused_computation | loop fusion | flops 262144 | bytes 2097152 | tf_op jit(solution)/shard_map/broadcast_in_dim | solution.py:398

commit v4 on v3

--- a/solution.py
+++ b/solution.py
@@ -297,9 +297,10 @@
                 for h in range(2):
                     encode(g[h][0, z], fs[h].at[0, z], fd.at[0, h, z], h)
                 gather_start(1, 0)
-            do = next(slots, None)
-            if do is not None:
-                do()
+            if m == 1 or hop < 2:
+                do = next(slots, None)
+                if do is not None:
+                    do()
     for h in range(2):
         encode(g[h][1, z], qb[h], qd.at[h], h)
     qd[...] = jnp.where(s > 0, qd[...], 0.0)

time: 114 us -> 113 us (level)
  no operation moved by 1% of the time
where the time goes in v4:
time: 113 us
  Pallas kernels  110 us (97%)
  other arithmetic  2.31 us (2%)
    pallas_call x1, Pallas kernels, run(): pl.pallas_call(kernel, out_shape=jax.ShapeDtypeStruct(warm.shape, jnp.flo...  110 us
    broadcast_in_dim x1, other arithmetic, local(): return (2.0 * refined)[None, :, None]  2.31 us

profile of v4, /device:TPU:16, one launch (start us, length us, event | category | flops | bytes accessed | tf_op | source)
XLA Modules:
  0.0 112.6 jit_solution(7335339279716734093)
XLA Ops:
  0.0 110.2 %factors.1 = f32[2,128,1024]{2,1,0:T(8,128)} custom-call(f32[2]{0:T(128)} %bitcast.12, s32[2]{0:T(128)} %bitcast.13, bf16[1024,1024]{1,0:T(8,128)(2,1)} %bitcast.9, bf16[1024,1024]{1,0:T(8,128)(2,1)} %bitcast.10, f32[2,128,1024]{2,1,0:T(8,128)} %bitcast.11), custom_call_target="tpu_custom_call" | custom-call | tf_op jit(solution)/shard_map/factors/pallas_call | solution.py:365
  110.2 2.3 %multiply_bitcast_fusion = f32[1,2,1,128,1024]{4,3,2,1,0:T(8,128)} fusion(f32[2,128,1024]{2,1,0:T(8,128)} %factors.1), kind=kLoop, calls=%fused_computation | loop fusion | flops 262144 | bytes 2097152 | tf_op jit(solution)/shard_map/broadcast_in_dim | solution.py:399
